TPU v7x, 256 devices: a whole 4x4x8 slice. The times are simulated.
256 devices in a mesh: cell: 32 (over y, x, core), lane: 8 (over z).
Axes of the slice: x: 4, y: 4, z: 8, core: 2. Of those that a mesh axis runs over, the one named last changes fastest.
Arguments:
- channel: float32 [32, 64, 2, 16, 256], P('cell', 'lane'), may hold values from -8 to 8
- symbols: bfloat16 [32, 16, 2, 2, 3072], P('cell'), may hold values from -4 to 4
- layers: int32 [32, 256], P('cell'), may hold values from 0 to 16, as said below
- user_ids: int32 [32, 16, 256], P('cell'), may hold values from 0 to 127
- user_power: float32 [32, 128], P('cell'), may hold values from 0.25 to 4
- neighbours: int32 [32, 6], replicated, may hold values from 0 to 31, as said below
- coupling: float32 [32, 6], replicated, may hold values from 0.05 to 0.5
Outputs:
- time_samples: float32 [32, 64, 2, 2, 4096], P('cell', 'lane')
Inputs may be any that keep to these rules, and one draw needn't show every extreme that they name: Some block of some cell has all 16 layers granted; for every index of the cell axis and every group of 8 aligned blocks, the layers of that index's 1 cells over the group sum to at most 48, and to exactly 48 for some index and group. `neighbours`: a cell never lists itself.
All inputs are finite; a program needn't handle non-finite values.
Results may differ from a plain program's by a relative error of at most 0.0029.
Values may be sent and summed in bfloat16 or wider, within the bound.
A program may use at most 64 MiB of HBM per device.

v0:
```python
import functools
import math

import jax
import jax.numpy as jnp
import numpy as np
from jax import lax
from jax.experimental import pallas as pl
from jax.experimental.pallas import tpu as pltpu
from jax.sharding import PartitionSpec as P

MESH = pl.DeviceIdType.MESH
NFFT = 4096
PRBS = 256
SUBC = 12
SYMS = 2
LAYERS = 16
NORM_EPS = 1e-06
NOISE_FLOOR = 0.05
LANES = 8
W = 128
F32 = jnp.float32
BF16 = jnp.bfloat16


def lanes_of(shape):
    return lax.broadcasted_iota(jnp.int32, shape, len(shape) - 1)


def swap4(x):
    lane = lanes_of(x[0].shape)
    low_half = lane < 64
    even = lax.rem(lane, 64) < 32
    y0 = jnp.where(low_half, x[0], pltpu.roll(x[2], 64, 1))
    y2 = jnp.where(low_half, pltpu.roll(x[0], 64, 1), x[2])
    y1 = jnp.where(low_half, x[1], pltpu.roll(x[3], 64, 1))
    y3 = jnp.where(low_half, pltpu.roll(x[1], 64, 1), x[3])
    z0 = jnp.where(even, y0, pltpu.roll(y1, 32, 1))
    z1 = jnp.where(even, pltpu.roll(y0, 96, 1), y1)
    z2 = jnp.where(even, y2, pltpu.roll(y3, 32, 1))
    z3 = jnp.where(even, pltpu.roll(y2, 96, 1), y3)
    return [z0, z1, z2, z3]


def pick4(x):
    lane = lanes_of(x[0].shape)
    return jnp.where(
        lane < 64,
        jnp.where(lane < 32, x[0], x[1]),
        jnp.where(lane < 96, x[2], x[3]),
    )


def spread4(x):
    r = [x, pltpu.roll(x, 32, 1), pltpu.roll(x, 64, 1), pltpu.roll(x, 96, 1)]
    return [pick4([r[(h - g) % 4] for h in range(4)]) for g in range(4)]


def total4(x):
    x = x + pltpu.roll(x, 64, 1)
    return x + pltpu.roll(x, 32, 1)


def solve_kernel(
    cells, ch, lay, uid, power, neigh, coup, w_out,
    sb, rb, amp, tx_own, tx_all, ea, ecol, scol, vs, wsb,
    hs, hr, ts, tr, ws, wr,
):
    me = lax.axis_index("lane")
    mc = lax.axis_index("cell")
    barrier = pltpu.get_barrier_semaphore()

    def lane_peer(d):
        return lax.rem(me + d, LANES)

    def cell_peer(d):
        return lax.rem(mc + d, cells)

    def greet_lane(d, _):
        pl.semaphore_signal(barrier, inc=1, device_id={"lane": lane_peer(d)}, device_id_type=MESH)
        return _

    def greet_cell(d, _):
        pl.semaphore_signal(barrier, inc=1, device_id={"cell": cell_peer(d)}, device_id_type=MESH)
        return _

    lax.fori_loop(1, LANES, greet_lane, 0)
    lax.fori_loop(1, cells, greet_cell, 0)

    root = jnp.broadcast_to(jnp.sqrt(power[...]), (LAYERS, W))
    layer = lax.broadcasted_iota(jnp.int32, (LAYERS, W), 0)
    for h in range(2):
        part = slice(h * W, (h + 1) * W)
        picked = jnp.take_along_axis(root, uid[:, part], axis=1, mode="promise_in_bounds")
        granted = layer < lay[:, part]
        spread = swap4([jnp.where(granted, picked, 0.0)] * 4)
        for q in range(4):
            amp[4 * h + q] = spread[q]
        mask = jnp.where(granted, 1.0, 0.0)
        for ah in range(2):
            for c in range(2):
                turned = swap4([ch[ah * 4 + g, c, :, part] * mask for g in range(4)])
                for q in range(4):
                    sb[2 * (4 * h + q) + ah, c] = turned[q]
    own_amp = amp[me]
    transmit = jnp.sum(own_amp * own_amp, axis=0, keepdims=True) / LAYERS
    tx_own[...] = transmit
    tx_all[mc] = transmit

    def tx_copy(d):
        return pltpu.make_async_remote_copy(
            src_ref=tx_own, dst_ref=tx_all.at[mc], send_sem=ts.at[d - 1], recv_sem=tr.at[d - 1],
            device_id={"cell": cell_peer(d)}, device_id_type=MESH,
        )

    def block_copy(src, dst, send, recv, d):
        return pltpu.make_async_remote_copy(
            src_ref=src.at[pl.ds(2 * lane_peer(d), 2)], dst_ref=dst.at[pl.ds(2 * me, 2)],
            send_sem=send.at[d - 1], recv_sem=recv.at[d - 1],
            device_id={"lane": lane_peer(d)}, device_id_type=MESH,
        )

    far_first = (4, 3, 5, 2, 6, 1, 7)
    pl.semaphore_wait(barrier, LANES - 1 + cells - 1)
    for d in far_first:
        block_copy(sb, rb, hs, hr, d).start()

    def start_tx(d, _):
        tx_copy(d).start()
        return _

    lax.fori_loop(1, cells, start_tx, 0)
    rb[pl.ds(2 * me, 2)] = sb[pl.ds(2 * me, 2)]

    def end_tx(d, _):
        tx_copy(d).wait()
        return _

    lax.fori_loop(1, cells, end_tx, 0)
    sigma = jnp.full((1, W), NOISE_FLOOR, F32)
    for k in range(neigh.shape[1]):
        sigma = sigma + coup[mc, k] * tx_all[neigh[mc, k]]
    for d in far_first[::-1]:
        block_copy(sb, rb, hs, hr, d).wait()

    zero = jnp.zeros((8, W), F32)
    for lt in range(2):
        rows = slice(8 * lt, 8 * lt + 8)

        def gram_step(a, acc, rows=rows):
            ar, ai = rb[a, 0, rows, :], rb[a, 1, rows, :]
            out = []
            for m in range(LAYERS):
                br, bi = rb[a, 0, m : m + 1, :], rb[a, 1, m : m + 1, :]
                out.append(acc[2 * m] + (ar * br + ai * bi))
                out.append(acc[2 * m + 1] + (ai * br - ar * bi))
            return tuple(out)

        acc = lax.fori_loop(0, 2 * LANES, gram_step, (zero,) * (2 * LAYERS))
        for m in range(LAYERS):
            ea[0, m, rows, :] = total4(acc[2 * m])
            ea[1, m, rows, :] = total4(acc[2 * m + 1])

    diagonal = jnp.zeros((LAYERS, W), F32)
    for m in range(LAYERS):
        diagonal = diagonal + jnp.where(layer == m, ea[0, m] + sigma, 0.0)
    inv_trace = 1.0 / jnp.sum(diagonal, axis=0, keepdims=True)
    for m in range(LAYERS):
        ea[0, m] = jnp.where(layer == m, 1.0 - (ea[0, m] + sigma) * inv_trace, -ea[0, m] * inv_trace)
        ea[1, m] = -ea[1, m] * inv_trace
    column = lanes_of((LAYERS, W)) // 32
    for j in range(4):
        for c in range(2):
            ecol[c, j] = pick4([ea[c, 4 * j + g] for g in range(4)])
        scol[0, j] = ecol[0, j] + jnp.where(layer == 4 * j + column, 1.0, 0.0)
        scol[1, j] = ecol[1, j]

    def products(refs):
        sums = [[[jnp.zeros((LAYERS, W), F32) for j in range(4)] for c in range(2)] for _ in refs]
        for k in range(LAYERS):
            ar, ai = ea[0, k], ea[1, k]
            for out, ref in zip(sums, refs):
                for j in range(4):
                    br, bi = ref[0, j, k : k + 1, :], ref[1, j, k : k + 1, :]
                    out[0][j] = out[0][j] + (ar * br - ai * bi)
                    out[1][j] = out[1][j] + (ar * bi + ai * br)
        return sums

    def put_square(square):
        for c in range(2):
            for j in range(4):
                ecol[c, j] = square[c][j]
                full = spread4(square[c][j])
                for g in range(4):
                    ea[c, 4 * j + g] = full[g]

    put_square(products([ecol])[0])

    def level(i, _):
        square, more = products([ecol, scol])
        for c in range(2):
            for j in range(4):
                scol[c, j] = scol[c, j] + more[c][j]
        put_square(square)
        return _

    lax.fori_loop(1, 5, level, 0)
    (more,) = products([scol])
    for c in range(2):
        for j in range(4):
            full = spread4((scol[c, j] + more[c][j]) * inv_trace)
            for g in range(4):
                ea[c, 4 * j + g] = full[g]

    def apply_step(z, energy):
        sums = [[jnp.zeros((LAYERS, W), F32) for c in range(2)] for ah in range(2)]
        for m in range(LAYERS):
            xr, xi = ea[0, m], ea[1, m]
            for ah in range(2):
                br, bi = rb[2 * z + ah, 0, m : m + 1, :], rb[2 * z + ah, 1, m : m + 1, :]
                sums[ah][0] = sums[ah][0] + (br * xr - bi * xi)
                sums[ah][1] = sums[ah][1] + (br * xi + bi * xr)
        for ah in range(2):
            vr, vi = sums[ah]
            vs[2 * z + ah, 0] = vr
            vs[2 * z + ah, 1] = -vi
            energy = energy + (vr * vr + vi * vi)
        return energy

    energy = total4(lax.fori_loop(0, LANES, apply_step, jnp.zeros((LAYERS, W), F32)))
    scale = own_amp / jnp.sqrt(energy + NORM_EPS)

    def round_step(a, _):
        for c in range(2):
            wsb[a, c] = (vs[a, c] * scale).astype(BF16)
        return _

    lax.fori_loop(0, 2 * LANES, round_step, 0)
    for d in far_first:
        block_copy(wsb, w_out, ws, wr, d).start()
    w_out[pl.ds(2 * me, 2)] = wsb[pl.ds(2 * me, 2)]
    for d in far_first[::-1]:
        block_copy(wsb, w_out, ws, wr, d).wait()


def solve(cells, channel, layers, user_ids, user_power, neighbours, coupling):
    vmem = pl.BlockSpec(memory_space=pltpu.VMEM)
    smem = pl.BlockSpec(memory_space=pltpu.SMEM)
    block = (2 * LANES, 2, LAYERS, W)
    dma = pltpu.SemaphoreType.DMA
    return pl.pallas_call(
        functools.partial(solve_kernel, cells),
        out_shape=jax.ShapeDtypeStruct(block, BF16),
        in_specs=[vmem] * 4 + [smem] * 2,
        out_specs=vmem,
        scratch_shapes=[
            pltpu.VMEM(block, F32),
            pltpu.VMEM(block, F32),
            pltpu.VMEM((LANES, LAYERS, W), F32),
            pltpu.VMEM((1, W), F32),
            pltpu.VMEM((cells, 1, W), F32),
            pltpu.VMEM((2, LAYERS, LAYERS, W), F32),
            pltpu.VMEM((2, 4, LAYERS, W), F32),
            pltpu.VMEM((2, 4, LAYERS, W), F32),
            pltpu.VMEM(block, F32),
            pltpu.VMEM(block, BF16),
            dma((LANES - 1,)),
            dma((LANES - 1,)),
            dma((cells - 1,)),
            dma((cells - 1,)),
            dma((LANES - 1,)),
            dma((LANES - 1,)),
        ],
        compiler_params=pltpu.CompilerParams(collective_id=0, has_side_effects=True),
        name="solve",
    )(channel, layers, user_ids, user_power, neighbours, coupling)


def ofdm_kernel(w, sym, dft, twist, out, tmp, sy, wn, gf, lhs):
    j = lax.broadcasted_iota(jnp.int32, (384, 384), 0)
    o = lax.broadcasted_iota(jnp.int32, (384, 384), 1)
    source = SUBC * lax.rem(o, 32) + o // 32
    order = jnp.where(j == source, 1.0, 0.0).astype(BF16)
    for z in range(8):
        tmp[z] = jnp.dot(sym[:, 384 * z : 384 * (z + 1)], order, preferred_element_type=F32)
    for h in range(2):
        for t in range(3):
            turned = swap4([tmp[4 * h + q, :, W * t : W * (t + 1)] for q in range(4)])
            for kk in range(4):
                k = 4 * t + kk
                for s in range(SYMS):
                    for b in range(4):
                        sy[h, pl.ds(b * 8 * 24 + s * SUBC + k, 8, stride=24), :] = turned[kk][
                            s * 32 + b * 8 : s * 32 + b * 8 + 8, :
                        ]
        for ah in range(2):
            for c in range(2):
                turned = swap4([w[2 * (4 * h + q) + ah, c].astype(F32) for q in range(4)])
                for g in range(4):
                    wn[h, ah * 4 + g, c] = turned[g]

    for h in range(2):

        def precode(half, _, h=h):
            sums = [[[jnp.zeros((8, W), F32) for i in range(3)] for c in range(2)] for a in range(4)]
            for l in range(LAYERS):
                sr = [sy[h, (2 * l) * 24 + 8 * i : (2 * l) * 24 + 8 * i + 8, :] for i in range(3)]
                si = [sy[h, (2 * l + 1) * 24 + 8 * i : (2 * l + 1) * 24 + 8 * i + 8, :] for i in range(3)]
                for a in range(4):
                    wr = wn[h, 4 * half + a, 0, l : l + 1, :]
                    wi = wn[h, 4 * half + a, 1, l : l + 1, :]
                    for i in range(3):
                        sums[a][0][i] = sums[a][0][i] + (wr * sr[i] - wi * si[i])
                        sums[a][1][i] = sums[a][1][i] + (wr * si[i] + wi * sr[i])
            for a in range(4):
                for c in range(2):
                    for i in range(3):
                        gf[c, h, pl.ds(64 * i + 4 * half + a, 8, stride=8), :] = sums[a][c][i]
            return _

        lax.fori_loop(0, 2, precode, 0)

    for c in range(2):
        for h in range(2):
            value = gf[c, h]
            high = value.astype(BF16)
            cols = slice(c * PRBS + h * W, c * PRBS + (h + 1) * W)
            lhs[0:192, cols] = high
            lhs[192:384, cols] = (value - high.astype(F32)).astype(BF16)

    def section(nt, _):
        result = jnp.dot(lhs[...], dft[nt], preferred_element_type=F32)
        result = result[0:192] + result[192:384]
        for s in range(SYMS):
            part = [[None, None] for _ in range(4)]
            for k in range(SUBC):
                row = (s * SUBC + k) * 8
                tr, ti = result[row : row + 8, 0:W], result[row : row + 8, W : 2 * W]
                cr, ci = twist[nt, k : k + 1, :], twist[nt, SUBC + k : SUBC + k + 1, :]
                ur, ui = tr * cr - ti * ci, tr * ci + ti * cr
                held = part[k % 4]
                held[0] = ur if held[0] is None else held[0] + ur
                held[1] = ui if held[1] is None else held[1] + ui
            (ar, ai), (br, bi), (cr, ci), (dr, di) = part
            pr, pi, mr, mi = ar + cr, ai + ci, ar - cr, ai - ci
            qr, qi, nr, ni = br + dr, bi + di, br - dr, bi - di
            outs = ((pr + qr, pi + qi), (mr - ni, mi + nr), (pr - qr, pi - qi), (mr + ni, mi - nr))
            for n2 in range(4):
                for c in range(2):
                    out[pl.ds(c * 64 + (n2 * 8 + nt) * 2 + s, 8, stride=128), :] = outs[n2][c]
        return _

    lax.fori_loop(0, 8, section, 0)


def ofdm_tables():
    p = np.arange(PRBS)[:, None]
    n = np.arange(1024)[None, :]
    angle = 2.0 * math.pi * ((3 * p * n) % 1024) / 1024
    cos, sin = np.cos(angle), np.sin(angle)
    real = np.concatenate([cos, -sin], 0).reshape(2 * PRBS, 8, 1, W)
    imag = np.concatenate([sin, cos], 0).reshape(2 * PRBS, 8, 1, W)
    dft = np.concatenate([real, imag], 2).reshape(2 * PRBS, 8, 2 * W).transpose(1, 0, 2)
    k = np.arange(SUBC)[:, None]
    angle = 2.0 * math.pi * (((k - 1536) * n) % NFFT) / NFFT
    twist = np.concatenate([np.cos(angle), np.sin(angle)], 0) / math.sqrt(NFFT)
    twist = twist.reshape(2 * SUBC, 8, W).transpose(1, 0, 2)
    return jnp.asarray(dft, BF16), jnp.asarray(twist, F32)


def ofdm(weights, symbols):
    vmem = pl.BlockSpec(memory_space=pltpu.VMEM)
    dft, twist = ofdm_tables()
    return pl.pallas_call(
        ofdm_kernel,
        out_shape=jax.ShapeDtypeStruct((1024, W), F32),
        in_specs=[vmem] * 4,
        out_specs=vmem,
        scratch_shapes=[
            pltpu.VMEM((8, 64, 384), F32),
            pltpu.VMEM((2, 768, W), F32),
            pltpu.VMEM((2, 8, 2, LAYERS, W), F32),
            pltpu.VMEM((2, 2, 192, W), F32),
            pltpu.VMEM((384, 512), BF16),
        ],
        name="ofdm",
    )(weights, symbols, dft, twist)


def per_device(cells, channel, symbols, layers, user_ids, user_power, neighbours, coupling):
    weights = solve(cells, channel[0], layers, user_ids[0], user_power, neighbours, coupling)
    rows = jnp.transpose(symbols[0], (2, 0, 1, 3)).reshape(64, 3072)
    samples = ofdm(weights, rows)
    samples = samples.reshape(8, 2, 32, SYMS, W).transpose(0, 1, 3, 2, 4)
    return samples.reshape(1, 8, 2, SYMS, NFFT)


def solution(mesh):
    in_specs = (
        P("cell", "lane", None, None, None),
        P("cell", None, None, None, None),
        P("cell", None),
        P("cell", None, None),
        P("cell", None),
        P(),
        P(),
    )
    out_specs = P("cell", "lane", None, None, None)
    return jax.shard_map(
        functools.partial(per_device, mesh.shape["cell"]),
        mesh=mesh, in_specs=in_specs, out_specs=out_specs, check_vma=False,
    )
```

profile of v0, /device:TPU:1, one launch (start us, length us, event | category | flops | bytes accessed | tf_op | source)
XLA Modules:
  0.0 42.0 jit_solution(2067526696533510016)
XLA Ops:
  0.0 1.4 %copy.10.neigh = s32[32,6]{1,0:T(8,128)} copy(s32[32,6]{0,1:T(8,128)} %param.14) | data formatting | bytes 1536 | tf_op args[5]
  1.4 1.4 %copy.11.coup = f32[32,6]{1,0:T(8,128)} copy(f32[32,6]{0,1:T(8,128)} %param.15) | data formatting | bytes 1536 | tf_op args[6]
  2.7 30.3 %solve.1.w = bf16[16,2,16,128]{3,2,1,0:T(8,128)(2,1)} custom-call(f32[8,2,16,256]{3,2,1,0:T(8,128)} %bitcast.11, s32[1,256]{1,0:T(1,128)} %lay.1, s32[16,256]{1,0:T(8,128)} %bitcast.12, f32[1,128]{1,0:T(1,128)} %power.1, s32[32,6]{1,0:T(8,128)} %copy.10.neigh, f32[32,6]{1,0:T(8,128)} %copy.11.coup), custom_call_target="tpu_custom_call" | custom-call | tf_op jit(solution)/shard_map/solve/pallas_call | solution.py:251
  33.0 1.3 %copy.12 = bf16[2,16,2,3072]{3,2,1,0:T(2,128)(2,1)S(1)} copy(bf16[2,16,2,3072]{3,0,2,1:T(2,128)(2,1)} %bitcast.10) | data formatting | bytes 786432 | tf_op jit(solution)/shard_map/transpose | solution.py:392
  34.3 0.9 %reshape.9.sym = bf16[64,3072]{1,0:T(8,128)(2,1)} reshape(bf16[2,16,2,3072]{3,2,1,0:T(2,128)(2,1)S(1)} %copy.12) | data formatting | bytes 786432 | tf_op jit(solution)/shard_map/reshape | solution.py:392
  35.2 6.7 %ofdm.1 = f32[1024,128]{1,0:T(8,128)} custom-call(bf16[16,2,16,128]{3,2,1,0:T(8,128)(2,1)} %solve.1.w, bf16[64,3072]{1,0:T(8,128)(2,1)} %reshape.9.sym, bf16[8,512,256]{2,1,0:T(8,128)(2,1)} %constant.4.clone.dft, f32[8,24,128]{2,1,0:T(8,128)} %constant.5.clone.twist), custom_call_target="tpu_custom_call" | custom-call | tf_op jit(solution)/shard_map/ofdm/pallas_call | solution.py:374
where the time goes:
time: 42.2 us; the launch traced here: 42 us
  Pallas kernels  37 us (88%)
  local copies, waits for them, and re-layouts  4.92 us (12%)
    pallas_call x1, Pallas kernels, solve(): pl.pallas_call(functools.partial(solve_kernel, cells), out_shape=jax.Shap...  30.3 us
    pallas_call x1, Pallas kernels, ofdm(): pl.pallas_call(ofdm_kernel, out_shape=jax.ShapeDtypeStruct((1024, W), F32...  6.75 us
    unnamed x2, local copies, waits for them, and re-layouts  2.73 us
    transpose x1, local copies, waits for them, and re-layouts, per_device(): rows = jnp.transpose(symbols[0], (2, 0, 1, 3)).reshape(64, 3072)  1.3 us
    reshape x1, local copies, waits for them, and re-layouts, per_device(): rows = jnp.transpose(symbols[0], (2, 0, 1, 3)).reshape(64, 3072)  0.89 us

commit v1 on v0

--- a/solution.py
+++ b/solution.py
@@ -61,11 +61,48 @@
     return x + pltpu.roll(x, 32, 1)
 
 
-def solve_kernel(
-    cells, ch, lay, uid, power, neigh, coup, w_out,
-    sb, rb, amp, tx_own, tx_all, ea, ecol, scol, vs, wsb,
-    hs, hr, ts, tr, ws, wr,
+def spread_symbols(sym, symf, tmp, sy):
+    def widen(lc, _):
+        pair = sym[lc].astype(F32)
+        symf[pl.ds(lc, 1), :] = pair[0:1, :]
+        symf[pl.ds(2 * LAYERS + lc, 1), :] = pair[1:2, :]
+        return _
+
+    lax.fori_loop(0, 2 * LAYERS, widen, 0)
+    j = lax.broadcasted_iota(jnp.int32, (384, 384), 0)
+    o = lax.broadcasted_iota(jnp.int32, (384, 384), 1)
+    source = SUBC * lax.rem(o, 32) + o // 32
+    order = jnp.where(j == source, 1.0, 0.0).astype(BF16)
+    for z in range(8):
+        tmp[z] = jnp.dot(symf[:, 384 * z : 384 * (z + 1)].astype(BF16), order, preferred_element_type=F32)
+    for h in range(2):
+        for t in range(3):
+            turned = swap4([tmp[4 * h + q, :, W * t : W * (t + 1)] for q in range(4)])
+            for kk in range(4):
+                k = 4 * t + kk
+                for s in range(SYMS):
+                    for b in range(4):
+                        sy[h, pl.ds(b * 8 * 24 + s * SUBC + k, 8, stride=24), :] = turned[kk][
+                            s * 32 + b * 8 : s * 32 + b * 8 + 8, :
+                        ]
+
+
+def slot_kernel(
+    cells, ch_any, sym_any, lay_any, uid_any, power_any, neigh_any, coup_any, dft_any, twist_any, out,
+    ch, sym, lay, uid, power, neigh, coup, dft, twist,
+    sb, rb, amp, tx_own, tx_all, ea, ecol, scol, vs, wsb, w_out,
+    symf, tmp, sy, wn, gf, lhs,
+    ins, hs, hr, ts, tr, ws, wr,
 ):
+    fetches = [
+        pltpu.make_async_copy(source, held, ins.at[i])
+        for i, (source, held) in enumerate((
+            (lay_any, lay), (uid_any, uid), (power_any, power), (ch_any, ch), (neigh_any, neigh),
+            (coup_any, coup), (sym_any, sym), (dft_any, dft), (twist_any, twist),
+        ))
+    ]
+    for fetch in fetches:
+        fetch.start()
     me = lax.axis_index("lane")
     mc = lax.axis_index("cell")
     barrier = pltpu.get_barrier_semaphore()
@@ -87,6 +124,8 @@
     lax.fori_loop(1, LANES, greet_lane, 0)
     lax.fori_loop(1, cells, greet_cell, 0)
 
+    for fetch in fetches[:4]:
+        fetch.wait()
     root = jnp.broadcast_to(jnp.sqrt(power[...]), (LAYERS, W))
     layer = lax.broadcasted_iota(jnp.int32, (LAYERS, W), 0)
     for h in range(2):
@@ -132,14 +171,19 @@
     lax.fori_loop(1, cells, start_tx, 0)
     rb[pl.ds(2 * me, 2)] = sb[pl.ds(2 * me, 2)]
 
+    fetches[6].wait()
+    spread_symbols(sym, symf, tmp, sy)
+
     def end_tx(d, _):
         tx_copy(d).wait()
         return _
 
     lax.fori_loop(1, cells, end_tx, 0)
+    fetches[4].wait()
+    fetches[5].wait()
     sigma = jnp.full((1, W), NOISE_FLOOR, F32)
-    for k in range(neigh.shape[1]):
-        sigma = sigma + coup[mc, k] * tx_all[neigh[mc, k]]
+    for k in range(neigh.shape[0]):
+        sigma = sigma + coup[k, mc] * tx_all[neigh[k, mc]]
     for d in far_first[::-1]:
         block_copy(sb, rb, hs, hr, d).wait()
 
@@ -242,60 +286,10 @@
     for d in far_first[::-1]:
         block_copy(wsb, w_out, ws, wr, d).wait()
 
-
-def solve(cells, channel, layers, user_ids, user_power, neighbours, coupling):
-    vmem = pl.BlockSpec(memory_space=pltpu.VMEM)
-    smem = pl.BlockSpec(memory_space=pltpu.SMEM)
-    block = (2 * LANES, 2, LAYERS, W)
-    dma = pltpu.SemaphoreType.DMA
-    return pl.pallas_call(
-        functools.partial(solve_kernel, cells),
-        out_shape=jax.ShapeDtypeStruct(block, BF16),
-        in_specs=[vmem] * 4 + [smem] * 2,
-        out_specs=vmem,
-        scratch_shapes=[
-            pltpu.VMEM(block, F32),
-            pltpu.VMEM(block, F32),
-            pltpu.VMEM((LANES, LAYERS, W), F32),
-            pltpu.VMEM((1, W), F32),
-            pltpu.VMEM((cells, 1, W), F32),
-            pltpu.VMEM((2, LAYERS, LAYERS, W), F32),
-            pltpu.VMEM((2, 4, LAYERS, W), F32),
-            pltpu.VMEM((2, 4, LAYERS, W), F32),
-            pltpu.VMEM(block, F32),
-            pltpu.VMEM(block, BF16),
-            dma((LANES - 1,)),
-            dma((LANES - 1,)),
-            dma((cells - 1,)),
-            dma((cells - 1,)),
-            dma((LANES - 1,)),
-            dma((LANES - 1,)),
-        ],
-        compiler_params=pltpu.CompilerParams(collective_id=0, has_side_effects=True),
-        name="solve",
-    )(channel, layers, user_ids, user_power, neighbours, coupling)
-
-
-def ofdm_kernel(w, sym, dft, twist, out, tmp, sy, wn, gf, lhs):
-    j = lax.broadcasted_iota(jnp.int32, (384, 384), 0)
-    o = lax.broadcasted_iota(jnp.int32, (384, 384), 1)
-    source = SUBC * lax.rem(o, 32) + o // 32
-    order = jnp.where(j == source, 1.0, 0.0).astype(BF16)
-    for z in range(8):
-        tmp[z] = jnp.dot(sym[:, 384 * z : 384 * (z + 1)], order, preferred_element_type=F32)
     for h in range(2):
-        for t in range(3):
-            turned = swap4([tmp[4 * h + q, :, W * t : W * (t + 1)] for q in range(4)])
-            for kk in range(4):
-                k = 4 * t + kk
-                for s in range(SYMS):
-                    for b in range(4):
-                        sy[h, pl.ds(b * 8 * 24 + s * SUBC + k, 8, stride=24), :] = turned[kk][
-                            s * 32 + b * 8 : s * 32 + b * 8 + 8, :
-                        ]
         for ah in range(2):
             for c in range(2):
-                turned = swap4([w[2 * (4 * h + q) + ah, c].astype(F32) for q in range(4)])
+                turned = swap4([w_out[2 * (4 * h + q) + ah, c].astype(F32) for q in range(4)])
                 for g in range(4):
                     wn[h, ah * 4 + g, c] = turned[g]
 
@@ -327,6 +321,9 @@
             cols = slice(c * PRBS + h * W, c * PRBS + (h + 1) * W)
             lhs[0:192, cols] = high
             lhs[192:384, cols] = (value - high.astype(F32)).astype(BF16)
+
+    fetches[7].wait()
+    fetches[8].wait()
 
     def section(nt, _):
         result = jnp.dot(lhs[...], dft[nt], preferred_element_type=F32)
@@ -368,29 +365,53 @@
     return jnp.asarray(dft, BF16), jnp.asarray(twist, F32)
 
 
-def ofdm(weights, symbols):
-    vmem = pl.BlockSpec(memory_space=pltpu.VMEM)
+def slot(cells, channel, symbols, layers, user_ids, user_power, neighbours, coupling):
     dft, twist = ofdm_tables()
+    args = (channel, symbols, layers, user_ids, user_power, neighbours, coupling, dft, twist)
+    block = (2 * LANES, 2, LAYERS, W)
+    dma = pltpu.SemaphoreType.DMA
+    held = [(pltpu.SMEM if i in (5, 6) else pltpu.VMEM)(x.shape, x.dtype) for i, x in enumerate(args)]
     return pl.pallas_call(
-        ofdm_kernel,
+        functools.partial(slot_kernel, cells),
         out_shape=jax.ShapeDtypeStruct((1024, W), F32),
-        in_specs=[vmem] * 4,
-        out_specs=vmem,
-        scratch_shapes=[
+        in_specs=[pl.BlockSpec(memory_space=pl.ANY)] * len(args),
+        out_specs=pl.BlockSpec(memory_space=pltpu.VMEM),
+        scratch_shapes=held + [
+            pltpu.VMEM(block, F32),
+            pltpu.VMEM(block, F32),
+            pltpu.VMEM((LANES, LAYERS, W), F32),
+            pltpu.VMEM((1, W), F32),
+            pltpu.VMEM((cells, 1, W), F32),
+            pltpu.VMEM((2, LAYERS, LAYERS, W), F32),
+            pltpu.VMEM((2, 4, LAYERS, W), F32),
+            pltpu.VMEM((2, 4, LAYERS, W), F32),
+            pltpu.VMEM(block, F32),
+            pltpu.VMEM(block, BF16),
+            pltpu.VMEM(block, BF16),
+            pltpu.VMEM((64, 3072), F32),
             pltpu.VMEM((8, 64, 384), F32),
             pltpu.VMEM((2, 768, W), F32),
             pltpu.VMEM((2, 8, 2, LAYERS, W), F32),
             pltpu.VMEM((2, 2, 192, W), F32),
             pltpu.VMEM((384, 512), BF16),
+            dma((len(args),)),
+            dma((LANES - 1,)),
+            dma((LANES - 1,)),
+            dma((cells - 1,)),
+            dma((cells - 1,)),
+            dma((LANES - 1,)),
+            dma((LANES - 1,)),
         ],
-        name="ofdm",
-    )(weights, symbols, dft, twist)
+        compiler_params=pltpu.CompilerParams(collective_id=0, has_side_effects=True),
+        name="slot",
+    )(*args)
 
 
 def per_device(cells, channel, symbols, layers, user_ids, user_power, neighbours, coupling):
-    weights = solve(cells, channel[0], layers, user_ids[0], user_power, neighbours, coupling)
-    rows = jnp.transpose(symbols[0], (2, 0, 1, 3)).reshape(64, 3072)
-    samples = ofdm(weights, rows)
+    samples = slot(
+        cells, channel[0], symbols[0].reshape(2 * LAYERS, SYMS, 3072), layers, user_ids[0], user_power,
+        neighbours.T, coupling.T,
+    )
     samples = samples.reshape(8, 2, 32, SYMS, W).transpose(0, 1, 3, 2, 4)
     return samples.reshape(1, 8, 2, SYMS, NFFT)
 

time: 42.2 us -> 34.9 us (0.83)
  Pallas kernels: 37 us -> 32.8 us
  local copies, waits for them, and re-layouts: 4.92 us -> 1.89 us
    pallas_call x2 -> x1, Pallas kernels: 37 us -> 32.8 us  [slot(): pl.pallas_call(functools.partial(slot_kernel, cells), out_shape=jax.Shape...]
    transpose x1 -> x0, local copies, waits for them, and re-layouts: 1.3 us -> none  [per_device(): rows = jnp.transpose(symbols[0], (2, 0, 1, 3)).reshape(64, 3072)]
    reshape x1 -> x0, local copies, waits for them, and re-layouts: 0.89 us -> none  [per_device(): rows = jnp.transpose(symbols[0], (2, 0, 1, 3)).reshape(64, 3072)]
    unnamed x2 -> x1, local copies, waits for them, and re-layouts: 2.73 us -> 1.89 us
where the time goes in v1:
time: 34.9 us; the launch traced here: 34.7 us
  Pallas kernels  32.8 us (94%)
  local copies, waits for them, and re-layouts  1.89 us (5%)
    pallas_call x1, Pallas kernels, slot(): pl.pallas_call(functools.partial(slot_kernel, cells), out_shape=jax.Shape...  32.8 us
    unnamed x1, local copies, waits for them, and re-layouts  1.89 us

profile of v1, /device:TPU:1, one launch (start us, length us, event | category | flops | bytes accessed | tf_op | source)
XLA Modules:
  0.0 34.7 jit_solution(227188107487813758)
XLA Ops:
  0.0 32.8 %slot.1 = f32[1024,128]{1,0:T(8,128)} custom-call(f32[8,2,16,256]{3,2,1,0:T(8,128)} %bitcast.12, bf16[32,2,3072]{2,1,0:T(2,128)(2,1)} %bitcast.11, s32[1,256]{1,0:T(1,128)} %lay_any.1, s32[16,256]{1,0:T(8,128)} %bitcast.13, f32[1,128]{1,0:T(1,128)} %power_any.1, s32[6,32]{1,0:T(8,128)} %bitcast.14, f32[6,32]{1,0:T(8,128)} %bitcast.15, ...), custom_call_target="tpu_custom_call" | custom-call | tf_op jit(solution)/shard_map/slot/pallas_call | solution.py:374
  32.8 1.9 %copy.12 = f32[1,8,2,2,4096]{4,3,2,1,0:T(2,128)} copy(f32[1,8,2,2,4096]{4,3,2,1,0:T(2,128)} %bitcast.10) | data formatting | bytes 1048576

commit v2 on v1

--- a/solution.py
+++ b/solution.py
@@ -90,9 +90,9 @@
 def slot_kernel(
     cells, ch_any, sym_any, lay_any, uid_any, power_any, neigh_any, coup_any, dft_any, twist_any, out,
     ch, sym, lay, uid, power, neigh, coup, dft, twist,
-    sb, rb, amp, tx_own, tx_all, ea, ecol, scol, vs, wsb, w_out,
+    sb, rb, amp, tx_own, tx_all, sig_all, sig_in, ea, ecol, scol, vs, wsb, w_out,
     symf, tmp, sy, wn, gf, lhs,
-    ins, hs, hr, ts, tr, ws, wr,
+    ins, hs, hr, ts, tr, ss, sr, ws, wr,
 ):
     fetches = [
         pltpu.make_async_copy(source, held, ins.at[i])
@@ -122,35 +122,50 @@
         return _
 
     lax.fori_loop(1, LANES, greet_lane, 0)
-    lax.fori_loop(1, cells, greet_cell, 0)
-
-    for fetch in fetches[:4]:
+    hub = me == 0
+
+    @pl.when(hub)
+    def _():
+        lax.fori_loop(1, cells, greet_cell, 0)
+
+
+    for fetch in fetches[:3]:
         fetch.wait()
     root = jnp.broadcast_to(jnp.sqrt(power[...]), (LAYERS, W))
     layer = lax.broadcasted_iota(jnp.int32, (LAYERS, W), 0)
+    masks = []
     for h in range(2):
         part = slice(h * W, (h + 1) * W)
         picked = jnp.take_along_axis(root, uid[:, part], axis=1, mode="promise_in_bounds")
         granted = layer < lay[:, part]
-        spread = swap4([jnp.where(granted, picked, 0.0)] * 4)
+        masks.append(jnp.where(granted, 1.0, 0.0))
+        amplitude = jnp.where(granted, picked, 0.0)
+        tx_own[h : h + 1, :] = jnp.sum(amplitude * amplitude, axis=0, keepdims=True) / LAYERS
+        spread = swap4([amplitude] * 4)
         for q in range(4):
             amp[4 * h + q] = spread[q]
-        mask = jnp.where(granted, 1.0, 0.0)
+
+    def tx_copy(d):
+        return pltpu.make_async_remote_copy(
+            src_ref=tx_own, dst_ref=tx_all.at[mc], send_sem=ts, recv_sem=tr,
+            device_id={"cell": cell_peer(d)}, device_id_type=MESH,
+        )
+
+    @pl.when(hub)
+    def _():
+        pl.semaphore_wait(barrier, LANES - 1 + cells - 1)
+        for d in range(1, cells):
+            tx_copy(d).start()
+
+    fetches[3].wait()
+    for h in range(2):
+        part = slice(h * W, (h + 1) * W)
         for ah in range(2):
             for c in range(2):
-                turned = swap4([ch[ah * 4 + g, c, :, part] * mask for g in range(4)])
+                turned = swap4([ch[ah * 4 + g, c, :, part] * masks[h] for g in range(4)])
                 for q in range(4):
                     sb[2 * (4 * h + q) + ah, c] = turned[q]
     own_amp = amp[me]
-    transmit = jnp.sum(own_amp * own_amp, axis=0, keepdims=True) / LAYERS
-    tx_own[...] = transmit
-    tx_all[mc] = transmit
-
-    def tx_copy(d):
-        return pltpu.make_async_remote_copy(
-            src_ref=tx_own, dst_ref=tx_all.at[mc], send_sem=ts.at[d - 1], recv_sem=tr.at[d - 1],
-            device_id={"cell": cell_peer(d)}, device_id_type=MESH,
-        )
 
     def block_copy(src, dst, send, recv, d):
         return pltpu.make_async_remote_copy(
@@ -159,31 +174,48 @@
             device_id={"lane": lane_peer(d)}, device_id_type=MESH,
         )
 
+    def sigma_copy(z):
+        return pltpu.make_async_remote_copy(
+            src_ref=sig_all.at[z], dst_ref=sig_in, send_sem=ss.at[z - 1], recv_sem=sr,
+            device_id={"lane": z}, device_id_type=MESH,
+        )
+
     far_first = (4, 3, 5, 2, 6, 1, 7)
-    pl.semaphore_wait(barrier, LANES - 1 + cells - 1)
+    @pl.when(me != 0)
+    def _():
+        pl.semaphore_wait(barrier, LANES - 1)
+
     for d in far_first:
         block_copy(sb, rb, hs, hr, d).start()
 
-    def start_tx(d, _):
-        tx_copy(d).start()
-        return _
-
-    lax.fori_loop(1, cells, start_tx, 0)
+    @pl.when(hub)
+    def _():
+        tx_all[mc] = tx_own[...]
+        fetches[4].wait()
+        fetches[5].wait()
+
+        arrived = tx_all.at[pl.ds(0, cells - 1)]
+        pltpu.make_async_copy(arrived, arrived, tr).wait()
+        sigma = jnp.full((2, W), NOISE_FLOOR, F32)
+        for k in range(neigh.shape[0]):
+            sigma = sigma + coup[k, mc] * tx_all[neigh[k, mc]]
+        for h in range(2):
+            spread = swap4([sigma[h : h + 1, :]] * 4)
+            for q in range(4):
+                sig_all[4 * h + q] = spread[q]
+        for z in far_first:
+            sigma_copy(z).start()
+        sig_in[...] = sig_all[0]
+
+    @pl.when(me != 0)
+    def _():
+        fetches[4].wait()
+        fetches[5].wait()
+
     rb[pl.ds(2 * me, 2)] = sb[pl.ds(2 * me, 2)]
-
     fetches[6].wait()
     spread_symbols(sym, symf, tmp, sy)
 
-    def end_tx(d, _):
-        tx_copy(d).wait()
-        return _
-
-    lax.fori_loop(1, cells, end_tx, 0)
-    fetches[4].wait()
-    fetches[5].wait()
-    sigma = jnp.full((1, W), NOISE_FLOOR, F32)
-    for k in range(neigh.shape[0]):
-        sigma = sigma + coup[k, mc] * tx_all[neigh[k, mc]]
     for d in far_first[::-1]:
         block_copy(sb, rb, hs, hr, d).wait()
 
@@ -205,6 +237,18 @@
             ea[0, m, rows, :] = total4(acc[2 * m])
             ea[1, m, rows, :] = total4(acc[2 * m + 1])
 
+    @pl.when(me != 0)
+    def _():
+        sigma_copy(1).wait_recv()
+
+    @pl.when(hub)
+    def _():
+        for z in range(1, LANES):
+            sigma_copy(z).wait_send()
+        arrived = tx_all.at[pl.ds(0, cells - 1)]
+        pltpu.make_async_copy(arrived, arrived, ts).wait()
+
+    sigma = sig_in[...]
     diagonal = jnp.zeros((LAYERS, W), F32)
     for m in range(LAYERS):
         diagonal = diagonal + jnp.where(layer == m, ea[0, m] + sigma, 0.0)
@@ -319,15 +363,13 @@
             value = gf[c, h]
             high = value.astype(BF16)
             cols = slice(c * PRBS + h * W, c * PRBS + (h + 1) * W)
-            lhs[0:192, cols] = high
-            lhs[192:384, cols] = (value - high.astype(F32)).astype(BF16)
+            lhs[:, cols] = high
 
     fetches[7].wait()
     fetches[8].wait()
 
     def section(nt, _):
         result = jnp.dot(lhs[...], dft[nt], preferred_element_type=F32)
-        result = result[0:192] + result[192:384]
         for s in range(SYMS):
             part = [[None, None] for _ in range(4)]
             for k in range(SUBC):
@@ -373,15 +415,17 @@
     held = [(pltpu.SMEM if i in (5, 6) else pltpu.VMEM)(x.shape, x.dtype) for i, x in enumerate(args)]
     return pl.pallas_call(
         functools.partial(slot_kernel, cells),
-        out_shape=jax.ShapeDtypeStruct((1024, W), F32),
+        out_shape=pltpu.VMEM((1024, W), F32),
         in_specs=[pl.BlockSpec(memory_space=pl.ANY)] * len(args),
         out_specs=pl.BlockSpec(memory_space=pltpu.VMEM),
         scratch_shapes=held + [
             pltpu.VMEM(block, F32),
             pltpu.VMEM(block, F32),
             pltpu.VMEM((LANES, LAYERS, W), F32),
+            pltpu.VMEM((2, W), F32),
+            pltpu.VMEM((cells, 2, W), F32),
+            pltpu.VMEM((LANES, 1, W), F32),
             pltpu.VMEM((1, W), F32),
-            pltpu.VMEM((cells, 1, W), F32),
             pltpu.VMEM((2, LAYERS, LAYERS, W), F32),
             pltpu.VMEM((2, 4, LAYERS, W), F32),
             pltpu.VMEM((2, 4, LAYERS, W), F32),
@@ -393,12 +437,14 @@
             pltpu.VMEM((2, 768, W), F32),
             pltpu.VMEM((2, 8, 2, LAYERS, W), F32),
             pltpu.VMEM((2, 2, 192, W), F32),
-            pltpu.VMEM((384, 512), BF16),
+            pltpu.VMEM((192, 512), BF16),
             dma((len(args),)),
             dma((LANES - 1,)),
             dma((LANES - 1,)),
-            dma((cells - 1,)),
-            dma((cells - 1,)),
+            dma,
+            dma,
+            dma((LANES - 1,)),
+            dma,
             dma((LANES - 1,)),
             dma((LANES - 1,)),
         ],

time: 34.9 us -> 30.9 us (0.89)
  Pallas kernels: 32.8 us -> 30 us
  local copies, waits for them, and re-layouts: 1.89 us -> 0.8 us
    pallas_call x1, Pallas kernels: 32.8 us -> 30 us  [slot(): pl.pallas_call(functools.partial(slot_kernel, cells), out_shape=pltpu.VME...]
    unnamed x1, local copies, waits for them, and re-layouts: 1.89 us -> 0.8 us
where the time goes in v2:
time: 30.9 us; the launch traced here: 30.8 us
  Pallas kernels  30 us (97%)
  local copies, waits for them, and re-layouts  0.8 us (3%)
    pallas_call x1, Pallas kernels, slot(): pl.pallas_call(functools.partial(slot_kernel, cells), out_shape=pltpu.VME...  30 us
    unnamed x1, local copies, waits for them, and re-layouts  0.8 us

profile of v2, /device:TPU:1, one launch (start us, length us, event | category | flops | bytes accessed | tf_op | source)
XLA Modules:
  0.0 30.8 jit_solution(5112880918475632855)
XLA Ops:
  0.0 30.0 %slot.1 = f32[1024,128]{1,0:T(8,128)S(1)} custom-call(f32[8,2,16,256]{3,2,1,0:T(8,128)} %bitcast.12, bf16[32,2,3072]{2,1,0:T(2,128)(2,1)} %bitcast.11, s32[1,256]{1,0:T(1,128)} %lay_any.1, s32[16,256]{1,0:T(8,128)} %bitcast.13, f32[1,128]{1,0:T(1,128)} %power_any.1, s32[6,32]{1,0:T(8,128)} %bitcast.14, f32[6,32]{1,0:T(8,128)} %bitcast.15, ...), custom_call_target="tpu_custom_call" | custom-call | tf_op jit(solution)/shard_map/slot/pallas_call | solution.py:416
  30.0 0.8 %copy.12 = f32[1,8,2,2,4096]{4,3,2,1,0:T(2,128)} copy(f32[1,8,2,2,4096]{4,3,2,1,0:T(2,128)S(1)} %bitcast.10) | data formatting | bytes 1048576

commit v3 on v2

--- a/solution.py
+++ b/solution.py
@@ -87,12 +87,86 @@
                         ]
 
 
+GROUP = 8
+PACK_ROWS = 6
+
+
+def group_total(x):
+    position = lax.rem(lanes_of(x.shape), GROUP)
+    for step in (1, 2, 4):
+        upper = lax.rem(position // step, 2) == 1
+        x = x + jnp.where(upper, pltpu.roll(x, step, 1), pltpu.roll(x, W - step, 1))
+    return x
+
+
+def pack_tables(count):
+    shape = (LAYERS, W)
+    layer = lax.broadcasted_iota(jnp.int32, shape, 0)
+    lane = lanes_of(shape)
+    position = lax.rem(lane, GROUP)
+    base = lane - position
+    granted = layer < count
+    one = jnp.where(granted, 1, 0)
+    rank = one
+    for step in (1, 2, 4):
+        rank = rank + jnp.where(position >= step, pltpu.roll(rank, step, 1), 0)
+    rank = rank - one
+    number = group_total(one)
+    offset = group_total(jnp.minimum(count, layer))
+    target = lax.rem(offset + rank, GROUP)
+    unpack_lane = base + target
+    turn = lax.rem(position - offset + LAYERS * GROUP, GROUP)
+    unpack_row = jnp.minimum((offset + turn) // GROUP, PACK_ROWS - 1)
+    marked = jnp.where(granted, target, GROUP)
+    pack_lane = lane
+    for step in range(GROUP):
+        if step == 0:
+            seen = marked
+        else:
+            seen = jnp.where(
+                position + step < GROUP, pltpu.roll(marked, W - step, 1), pltpu.roll(marked, GROUP - step, 1)
+            )
+        source = base + lax.rem(position + step, GROUP)
+        pack_lane = jnp.where(seen == position, source, pack_lane)
+    row = lax.broadcasted_iota(jnp.int32, (8, W), 0)
+    pack_layer = jnp.zeros((8, W), jnp.int32)
+    for r in range(PACK_ROWS):
+        passed = jnp.where(offset + number <= GROUP * r + position, 1, 0)
+        level = jnp.minimum(jnp.sum(passed, axis=0, keepdims=True), LAYERS - 1)
+        pack_layer = jnp.where(row == r, level, pack_layer)
+    return granted, pack_lane, pack_layer, unpack_row, unpack_lane
+
+
+def along(x, index, axis):
+    return jnp.take_along_axis(x, index, axis=axis, mode="promise_in_bounds")
+
+
+def pack(x, tables):
+    pack_lane, pack_layer = tables[1], tables[2]
+    turned = [along(x[8 * i : 8 * i + 8], pack_lane[8 * i : 8 * i + 8], 1) for i in range(2)]
+    within = lax.rem(pack_layer, 8)
+    return jnp.where(pack_layer < 8, along(turned[0], within, 0), along(turned[1], within, 0))
+
+
+def unpack(x, tables, first=0):
+    granted, unpack_row, unpack_lane = tables[0], tables[3] + first, tables[4]
+    parts = []
+    for i in range(2):
+        rows = slice(8 * i, 8 * i + 8)
+        parts.append(along(along(x, unpack_row[rows], 0), unpack_lane[rows], 1))
+    return jnp.where(granted, jnp.concatenate(parts, axis=0), 0.0)
+
+
+def packed_start(i):
+    return min(PACK_ROWS * i, 4 * PACK_ROWS - 8)
+
+
 def slot_kernel(
     cells, ch_any, sym_any, lay_any, uid_any, power_any, neigh_any, coup_any, dft_any, twist_any, out,
     ch, sym, lay, uid, power, neigh, coup, dft, twist,
-    sb, rb, amp, tx_own, tx_all, sig_all, sig_in, ea, ecol, scol, vs, wsb, w_out,
+    sb, rb, hb, amp, lay_all, wsf, wrf, tx_own, tx_all, sig_all, sig_in, ea, ecol, scol, vs, wsb, w_out,
     symf, tmp, sy, wn, gf, lhs,
-    ins, hs, hr, ts, tr, ss, sr, ws, wr,
+    ins, hs, hr, ts, tr, ss, sr, ws, wr, ready,
 ):
     fetches = [
         pltpu.make_async_copy(source, held, ins.at[i])
@@ -113,17 +187,22 @@
     def cell_peer(d):
         return lax.rem(mc + d, cells)
 
-    def greet_lane(d, _):
-        pl.semaphore_signal(barrier, inc=1, device_id={"lane": lane_peer(d)}, device_id_type=MESH)
-        return _
+    hub = me == 0
+
+    def greet_lane(d, carry):
+        peer = lane_peer(d)
+
+        @pl.when(peer != 0)
+        def _():
+            pl.semaphore_signal(barrier, inc=1, device_id={"lane": peer}, device_id_type=MESH)
+
+        return carry
 
     def greet_cell(d, _):
         pl.semaphore_signal(barrier, inc=1, device_id={"cell": cell_peer(d)}, device_id_type=MESH)
         return _
 
     lax.fori_loop(1, LANES, greet_lane, 0)
-    hub = me == 0
-
     @pl.when(hub)
     def _():
         lax.fori_loop(1, cells, greet_cell, 0)
@@ -133,12 +212,13 @@
         fetch.wait()
     root = jnp.broadcast_to(jnp.sqrt(power[...]), (LAYERS, W))
     layer = lax.broadcasted_iota(jnp.int32, (LAYERS, W), 0)
-    masks = []
     for h in range(2):
         part = slice(h * W, (h + 1) * W)
         picked = jnp.take_along_axis(root, uid[:, part], axis=1, mode="promise_in_bounds")
         granted = layer < lay[:, part]
-        masks.append(jnp.where(granted, 1.0, 0.0))
+        spread = swap4([lay[:, part]] * 4)
+        for q in range(4):
+            lay_all[4 * h + q] = spread[q]
         amplitude = jnp.where(granted, picked, 0.0)
         tx_own[h : h + 1, :] = jnp.sum(amplitude * amplitude, axis=0, keepdims=True) / LAYERS
         spread = swap4([amplitude] * 4)
@@ -153,23 +233,25 @@
 
     @pl.when(hub)
     def _():
-        pl.semaphore_wait(barrier, LANES - 1 + cells - 1)
+        pl.semaphore_wait(barrier, cells - 1)
         for d in range(1, cells):
             tx_copy(d).start()
 
+    natural = [pack_tables(lay[:, h * W : (h + 1) * W]) for h in range(2)]
     fetches[3].wait()
     for h in range(2):
         part = slice(h * W, (h + 1) * W)
         for ah in range(2):
             for c in range(2):
-                turned = swap4([ch[ah * 4 + g, c, :, part] * masks[h] for g in range(4)])
+                turned = swap4([pack(ch[ah * 4 + g, c, :, part], natural[h]) for g in range(4)])
+                first = PACK_ROWS * (2 * ah + c)
                 for q in range(4):
-                    sb[2 * (4 * h + q) + ah, c] = turned[q]
+                    sb[4 * h + q, first : first + PACK_ROWS, :] = turned[q][:PACK_ROWS]
     own_amp = amp[me]
 
     def block_copy(src, dst, send, recv, d):
         return pltpu.make_async_remote_copy(
-            src_ref=src.at[pl.ds(2 * lane_peer(d), 2)], dst_ref=dst.at[pl.ds(2 * me, 2)],
+            src_ref=src.at[lane_peer(d)], dst_ref=dst.at[me],
             send_sem=send.at[d - 1], recv_sem=recv.at[d - 1],
             device_id={"lane": lane_peer(d)}, device_id_type=MESH,
         )
@@ -181,9 +263,15 @@
         )
 
     far_first = (4, 3, 5, 2, 6, 1, 7)
+    @pl.when(hub)
+    def _():
+        pl.semaphore_wait(ready, LANES - 1)
+
     @pl.when(me != 0)
     def _():
         pl.semaphore_wait(barrier, LANES - 1)
+
+        pl.semaphore_signal(ready, inc=1, device_id={"lane": 0}, device_id_type=MESH)
 
     for d in far_first:
         block_copy(sb, rb, hs, hr, d).start()
@@ -212,22 +300,34 @@
         fetches[4].wait()
         fetches[5].wait()
 
-    rb[pl.ds(2 * me, 2)] = sb[pl.ds(2 * me, 2)]
+    own_tables = pack_tables(lay_all[me])
+
+    def unpack_block(source, z):
+        for ah in range(2):
+            for c in range(2):
+                i = 2 * ah + c
+                first = packed_start(i)
+                hb[2 * z + ah, c] = unpack(
+                    source[z, first : first + 8, :], own_tables, PACK_ROWS * i - first
+                )
+
+    unpack_block(sb, me)
     fetches[6].wait()
     spread_symbols(sym, symf, tmp, sy)
 
     for d in far_first[::-1]:
         block_copy(sb, rb, hs, hr, d).wait()
+        unpack_block(rb, lax.rem(me - d + LANES, LANES))
 
     zero = jnp.zeros((8, W), F32)
     for lt in range(2):
         rows = slice(8 * lt, 8 * lt + 8)
 
         def gram_step(a, acc, rows=rows):
-            ar, ai = rb[a, 0, rows, :], rb[a, 1, rows, :]
+            ar, ai = hb[a, 0, rows, :], hb[a, 1, rows, :]
             out = []
             for m in range(LAYERS):
-                br, bi = rb[a, 0, m : m + 1, :], rb[a, 1, m : m + 1, :]
+                br, bi = hb[a, 0, m : m + 1, :], hb[a, 1, m : m + 1, :]
                 out.append(acc[2 * m] + (ar * br + ai * bi))
                 out.append(acc[2 * m + 1] + (ai * br - ar * bi))
             return tuple(out)
@@ -305,7 +405,7 @@
         for m in range(LAYERS):
             xr, xi = ea[0, m], ea[1, m]
             for ah in range(2):
-                br, bi = rb[2 * z + ah, 0, m : m + 1, :], rb[2 * z + ah, 1, m : m + 1, :]
+                br, bi = hb[2 * z + ah, 0, m : m + 1, :], hb[2 * z + ah, 1, m : m + 1, :]
                 sums[ah][0] = sums[ah][0] + (br * xr - bi * xi)
                 sums[ah][1] = sums[ah][1] + (br * xi + bi * xr)
         for ah in range(2):
@@ -318,24 +418,31 @@
     energy = total4(lax.fori_loop(0, LANES, apply_step, jnp.zeros((LAYERS, W), F32)))
     scale = own_amp / jnp.sqrt(energy + NORM_EPS)
 
-    def round_step(a, _):
-        for c in range(2):
-            wsb[a, c] = (vs[a, c] * scale).astype(BF16)
-        return _
-
-    lax.fori_loop(0, 2 * LANES, round_step, 0)
+    def round_block(z, target):
+        for ah in range(2):
+            for c in range(2):
+                first = PACK_ROWS * (2 * ah + c)
+                wsf[z, first : first + PACK_ROWS, :] = pack(vs[2 * z + ah, c] * scale, own_tables)[:PACK_ROWS]
+        target[z] = wsf[z].astype(BF16)
+
     for d in far_first:
+        round_block(lane_peer(d), wsb)
         block_copy(wsb, w_out, ws, wr, d).start()
-    w_out[pl.ds(2 * me, 2)] = wsb[pl.ds(2 * me, 2)]
+    round_block(me, w_out)
+    natural = [pack_tables(lay[:, h * W : (h + 1) * W]) for h in range(2)]
     for d in far_first[::-1]:
         block_copy(wsb, w_out, ws, wr, d).wait()
+    for z in range(LANES):
+        wrf[z] = w_out[z].astype(F32)
 
     for h in range(2):
         for ah in range(2):
             for c in range(2):
-                turned = swap4([w_out[2 * (4 * h + q) + ah, c].astype(F32) for q in range(4)])
+                i = 2 * ah + c
+                first = packed_start(i)
+                turned = swap4([wrf[4 * h + q, first : first + 8, :] for q in range(4)])
                 for g in range(4):
-                    wn[h, ah * 4 + g, c] = turned[g]
+                    wn[h, ah * 4 + g, c] = unpack(turned[g], natural[h], PACK_ROWS * i - first)
 
     for h in range(2):
 
@@ -411,6 +518,7 @@
     dft, twist = ofdm_tables()
     args = (channel, symbols, layers, user_ids, user_power, neighbours, coupling, dft, twist)
     block = (2 * LANES, 2, LAYERS, W)
+    packed = (LANES, 4 * PACK_ROWS, W)
     dma = pltpu.SemaphoreType.DMA
     held = [(pltpu.SMEM if i in (5, 6) else pltpu.VMEM)(x.shape, x.dtype) for i, x in enumerate(args)]
     return pl.pallas_call(
@@ -419,9 +527,13 @@
         in_specs=[pl.BlockSpec(memory_space=pl.ANY)] * len(args),
         out_specs=pl.BlockSpec(memory_space=pltpu.VMEM),
         scratch_shapes=held + [
-            pltpu.VMEM(block, F32),
+            pltpu.VMEM(packed, F32),
+            pltpu.VMEM(packed, F32),
             pltpu.VMEM(block, F32),
             pltpu.VMEM((LANES, LAYERS, W), F32),
+            pltpu.VMEM((LANES, 1, W), jnp.int32),
+            pltpu.VMEM(packed, F32),
+            pltpu.VMEM(packed, F32),
             pltpu.VMEM((2, W), F32),
             pltpu.VMEM((cells, 2, W), F32),
             pltpu.VMEM((LANES, 1, W), F32),
@@ -430,8 +542,8 @@
             pltpu.VMEM((2, 4, LAYERS, W), F32),
             pltpu.VMEM((2, 4, LAYERS, W), F32),
             pltpu.VMEM(block, F32),
-            pltpu.VMEM(block, BF16),
-            pltpu.VMEM(block, BF16),
+            pltpu.VMEM(packed, BF16),
+            pltpu.VMEM(packed, BF16),
             pltpu.VMEM((64, 3072), F32),
             pltpu.VMEM((8, 64, 384), F32),
             pltpu.VMEM((2, 768, W), F32),
@@ -447,6 +559,7 @@
             dma,
             dma((LANES - 1,)),
             dma((LANES - 1,)),
+            pltpu.SemaphoreType.REGULAR,
         ],
         compiler_params=pltpu.CompilerParams(collective_id=0, has_side_effects=True),
         name="slot",

time: 30.9 us -> 27.3 us (0.88)
  the two profiles are of different devices: /device:TPU:1 before, /device:TPU:6 now
where the time goes in v3:
time: 27.3 us
  Pallas kernels  26.4 us (97%)
  local copies, waits for them, and re-layouts  0.8 us (3%)
    pallas_call x1, Pallas kernels, slot(): pl.pallas_call(functools.partial(slot_kernel, cells), out_shape=pltpu.VME...  26.4 us
    unnamed x1, local copies, waits for them, and re-layouts  0.8 us

profile of v3, /device:TPU:6, one launch (start us, length us, event | category | flops | bytes accessed | tf_op | source)
XLA Modules:
  0.0 27.3 jit_solution(4053355007314391574)
XLA Ops:
  0.0 26.4 %slot.1 = f32[1024,128]{1,0:T(8,128)S(1)} custom-call(f32[8,2,16,256]{3,2,1,0:T(8,128)} %bitcast.12, bf16[32,2,3072]{2,1,0:T(2,128)(2,1)} %bitcast.11, s32[1,256]{1,0:T(1,128)} %lay_any.1, s32[16,256]{1,0:T(8,128)} %bitcast.13, f32[1,128]{1,0:T(1,128)} %power_any.1, s32[6,32]{1,0:T(8,128)} %bitcast.14, f32[6,32]{1,0:T(8,128)} %bitcast.15, ...), custom_call_target="tpu_custom_call" | custom-call | tf_op jit(solution)/shard_map/slot/pallas_call | solution.py:524
  26.5 0.8 %copy.12 = f32[1,8,2,2,4096]{4,3,2,1,0:T(2,128)} copy(f32[1,8,2,2,4096]{4,3,2,1,0:T(2,128)S(1)} %bitcast.10) | data formatting | bytes 1048576

commit v4 on v3

--- a/solution.py
+++ b/solution.py
@@ -64,8 +64,9 @@
 def spread_symbols(sym, symf, tmp, sy):
     def widen(lc, _):
         pair = sym[lc].astype(F32)
-        symf[pl.ds(lc, 1), :] = pair[0:1, :]
-        symf[pl.ds(2 * LAYERS + lc, 1), :] = pair[1:2, :]
+        row = lax.rem(lc, 2) * LAYERS + lc // 2
+        symf[pl.ds(row, 1), :] = pair[0:1, :]
+        symf[pl.ds(2 * LAYERS + row, 1), :] = pair[1:2, :]
         return _
 
     lax.fori_loop(0, 2 * LAYERS, widen, 0)
@@ -81,10 +82,10 @@
             for kk in range(4):
                 k = 4 * t + kk
                 for s in range(SYMS):
-                    for b in range(4):
-                        sy[h, pl.ds(b * 8 * 24 + s * SUBC + k, 8, stride=24), :] = turned[kk][
-                            s * 32 + b * 8 : s * 32 + b * 8 + 8, :
-                        ]
+                    parts = [turned[kk][s * 32 + b * 8 : s * 32 + b * 8 + 8, :] for b in range(4)]
+                    parts += [parts[0] + parts[2], parts[1] + parts[3]]
+                    for b, part in enumerate(parts):
+                        sy[h, pl.ds(b * 8 * 24 + s * SUBC + k, 8, stride=24), :] = part
 
 
 GROUP = 8
@@ -310,14 +311,20 @@
                 hb[2 * z + ah, c] = unpack(
                     source[z, first : first + 8, :], own_tables, PACK_ROWS * i - first
                 )
+            hb[2 * z + ah, 2] = hb[2 * z + ah, 0] + hb[2 * z + ah, 1]
 
     unpack_block(sb, me)
     fetches[6].wait()
     spread_symbols(sym, symf, tmp, sy)
 
-    for d in far_first[::-1]:
-        block_copy(sb, rb, hs, hr, d).wait()
-        unpack_block(rb, lax.rem(me - d + LANES, LANES))
+    def take_block(z):
+        @pl.when(me != z)
+        def _():
+            block_copy(sb, rb, hs, hr, lax.rem(me - z + LANES, LANES)).wait_recv()
+            unpack_block(rb, z)
+
+    for z in range(1, LANES):
+        take_block(z)
 
     zero = jnp.zeros((8, W), F32)
     for lt in range(2):
@@ -332,10 +339,23 @@
                 out.append(acc[2 * m + 1] + (ai * br - ar * bi))
             return tuple(out)
 
-        acc = lax.fori_loop(0, 2 * LANES, gram_step, (zero,) * (2 * LAYERS))
+        acc = lax.fori_loop(2, 2 * LANES, gram_step, (zero,) * (2 * LAYERS))
         for m in range(LAYERS):
-            ea[0, m, rows, :] = total4(acc[2 * m])
-            ea[1, m, rows, :] = total4(acc[2 * m + 1])
+            ea[0, m, rows, :] = acc[2 * m]
+            ea[1, m, rows, :] = acc[2 * m + 1]
+
+    take_block(0)
+    for lt in range(2):
+        rows = slice(8 * lt, 8 * lt + 8)
+        for m in range(LAYERS):
+            gr, gi = ea[0, m, rows, :], ea[1, m, rows, :]
+            for a in range(2):
+                ar, ai = hb[a, 0, rows, :], hb[a, 1, rows, :]
+                br, bi = hb[a, 0, m : m + 1, :], hb[a, 1, m : m + 1, :]
+                gr = gr + (ar * br + ai * bi)
+                gi = gi + (ai * br - ar * bi)
+            ea[0, m, rows, :] = total4(gr)
+            ea[1, m, rows, :] = total4(gi)
 
     @pl.when(me != 0)
     def _():
@@ -356,62 +376,72 @@
     for m in range(LAYERS):
         ea[0, m] = jnp.where(layer == m, 1.0 - (ea[0, m] + sigma) * inv_trace, -ea[0, m] * inv_trace)
         ea[1, m] = -ea[1, m] * inv_trace
+        ea[2, m] = ea[0, m] + ea[1, m]
     column = lanes_of((LAYERS, W)) // 32
     for j in range(4):
         for c in range(2):
             ecol[c, j] = pick4([ea[c, 4 * j + g] for g in range(4)])
         scol[0, j] = ecol[0, j] + jnp.where(layer == 4 * j + column, 1.0, 0.0)
         scol[1, j] = ecol[1, j]
-
-    def products(refs):
-        sums = [[[jnp.zeros((LAYERS, W), F32) for j in range(4)] for c in range(2)] for _ in refs]
+        ecol[2, j] = ecol[0, j] + ecol[1, j]
+        scol[2, j] = scol[0, j] + scol[1, j]
+
+    def product(ref):
+        sums = [[jnp.zeros((LAYERS, W), F32) for j in range(4)] for c in range(3)]
         for k in range(LAYERS):
-            ar, ai = ea[0, k], ea[1, k]
-            for out, ref in zip(sums, refs):
+            for c in range(3):
+                left = ea[c, k]
                 for j in range(4):
-                    br, bi = ref[0, j, k : k + 1, :], ref[1, j, k : k + 1, :]
-                    out[0][j] = out[0][j] + (ar * br - ai * bi)
-                    out[1][j] = out[1][j] + (ar * bi + ai * br)
-        return sums
+                    sums[c][j] = sums[c][j] + left * ref[c, j, k : k + 1, :]
+        real = [sums[0][j] - sums[1][j] for j in range(4)]
+        imag = [sums[2][j] - (sums[0][j] + sums[1][j]) for j in range(4)]
+        return real, imag
 
     def put_square(square):
         for c in range(2):
             for j in range(4):
                 ecol[c, j] = square[c][j]
-                full = spread4(square[c][j])
+        for j in range(4):
+            ecol[2, j] = square[0][j] + square[1][j]
+        for c in range(3):
+            for j in range(4):
+                full = spread4(ecol[c, j])
                 for g in range(4):
                     ea[c, 4 * j + g] = full[g]
 
-    put_square(products([ecol])[0])
+    put_square(product(ecol))
 
     def level(i, _):
-        square, more = products([ecol, scol])
-        for c in range(2):
-            for j in range(4):
+        more = product(scol)
+        square = product(ecol)
+        for j in range(4):
+            for c in range(2):
                 scol[c, j] = scol[c, j] + more[c][j]
+            scol[2, j] = scol[0, j] + scol[1, j]
         put_square(square)
         return _
 
     lax.fori_loop(1, 5, level, 0)
-    (more,) = products([scol])
-    for c in range(2):
-        for j in range(4):
-            full = spread4((scol[c, j] + more[c][j]) * inv_trace)
+    more = product(scol)
+    for j in range(4):
+        last = [(scol[c, j] + more[c][j]) * inv_trace for c in range(2)]
+        for c, part in enumerate(last + [last[0] + last[1]]):
+            full = spread4(part)
             for g in range(4):
                 ea[c, 4 * j + g] = full[g]
 
     def apply_step(z, energy):
-        sums = [[jnp.zeros((LAYERS, W), F32) for c in range(2)] for ah in range(2)]
+        sums = [[jnp.zeros((LAYERS, W), F32) for c in range(3)] for ah in range(2)]
         for m in range(LAYERS):
-            xr, xi = ea[0, m], ea[1, m]
-            for ah in range(2):
-                br, bi = hb[2 * z + ah, 0, m : m + 1, :], hb[2 * z + ah, 1, m : m + 1, :]
-                sums[ah][0] = sums[ah][0] + (br * xr - bi * xi)
-                sums[ah][1] = sums[ah][1] + (br * xi + bi * xr)
+            for c in range(3):
+                right = ea[c, m]
+                for ah in range(2):
+                    sums[ah][c] = sums[ah][c] + hb[2 * z + ah, c, m : m + 1, :] * right
         for ah in range(2):
-            vr, vi = sums[ah]
+            vr = sums[ah][0] - sums[ah][1]
+            vi = (sums[ah][0] + sums[ah][1]) - sums[ah][2]
             vs[2 * z + ah, 0] = vr
-            vs[2 * z + ah, 1] = -vi
+            vs[2 * z + ah, 1] = vi
             energy = energy + (vr * vr + vi * vi)
         return energy
 
@@ -432,6 +462,8 @@
     natural = [pack_tables(lay[:, h * W : (h + 1) * W]) for h in range(2)]
     for d in far_first[::-1]:
         block_copy(wsb, w_out, ws, wr, d).wait()
+    for d in far_first:
+        block_copy(sb, rb, hs, hr, d).wait_send()
     for z in range(LANES):
         wrf[z] = w_out[z].astype(F32)
 
@@ -443,20 +475,26 @@
                 turned = swap4([wrf[4 * h + q, first : first + 8, :] for q in range(4)])
                 for g in range(4):
                     wn[h, ah * 4 + g, c] = unpack(turned[g], natural[h], PACK_ROWS * i - first)
+            for g in range(4):
+                wn[h, ah * 4 + g, 2] = wn[h, ah * 4 + g, 0] + wn[h, ah * 4 + g, 1]
 
     for h in range(2):
 
         def precode(half, _, h=h):
-            sums = [[[jnp.zeros((8, W), F32) for i in range(3)] for c in range(2)] for a in range(4)]
+            sums = [[[jnp.zeros((8, W), F32) for i in range(3)] for c in range(3)] for a in range(4)]
             for l in range(LAYERS):
-                sr = [sy[h, (2 * l) * 24 + 8 * i : (2 * l) * 24 + 8 * i + 8, :] for i in range(3)]
-                si = [sy[h, (2 * l + 1) * 24 + 8 * i : (2 * l + 1) * 24 + 8 * i + 8, :] for i in range(3)]
-                for a in range(4):
-                    wr = wn[h, 4 * half + a, 0, l : l + 1, :]
-                    wi = wn[h, 4 * half + a, 1, l : l + 1, :]
-                    for i in range(3):
-                        sums[a][0][i] = sums[a][0][i] + (wr * sr[i] - wi * si[i])
-                        sums[a][1][i] = sums[a][1][i] + (wr * si[i] + wi * sr[i])
+                for c in range(3):
+                    first = (c * LAYERS + l) * 24
+                    right = [sy[h, first + 8 * i : first + 8 * i + 8, :] for i in range(3)]
+                    for a in range(4):
+                        left = wn[h, 4 * half + a, c, l : l + 1, :]
+                        for i in range(3):
+                            sums[a][c][i] = sums[a][c][i] + left * right[i]
+            for a in range(4):
+                for i in range(3):
+                    p0, p1, p2 = sums[a][0][i], sums[a][1][i], sums[a][2][i]
+                    sums[a][0][i] = p0 - p1
+                    sums[a][1][i] = p2 - (p0 + p1)
             for a in range(4):
                 for c in range(2):
                     for i in range(3):
@@ -529,7 +567,7 @@
         scratch_shapes=held + [
             pltpu.VMEM(packed, F32),
             pltpu.VMEM(packed, F32),
-            pltpu.VMEM(block, F32),
+            pltpu.VMEM((2 * LANES, 3, LAYERS, W), F32),
             pltpu.VMEM((LANES, LAYERS, W), F32),
             pltpu.VMEM((LANES, 1, W), jnp.int32),
             pltpu.VMEM(packed, F32),
@@ -538,16 +576,16 @@
             pltpu.VMEM((cells, 2, W), F32),
             pltpu.VMEM((LANES, 1, W), F32),
             pltpu.VMEM((1, W), F32),
-            pltpu.VMEM((2, LAYERS, LAYERS, W), F32),
-            pltpu.VMEM((2, 4, LAYERS, W), F32),
-            pltpu.VMEM((2, 4, LAYERS, W), F32),
+            pltpu.VMEM((3, LAYERS, LAYERS, W), F32),
+            pltpu.VMEM((3, 4, LAYERS, W), F32),
+            pltpu.VMEM((3, 4, LAYERS, W), F32),
             pltpu.VMEM(block, F32),
             pltpu.VMEM(packed, BF16),
             pltpu.VMEM(packed, BF16),
             pltpu.VMEM((64, 3072), F32),
             pltpu.VMEM((8, 64, 384), F32),
-            pltpu.VMEM((2, 768, W), F32),
-            pltpu.VMEM((2, 8, 2, LAYERS, W), F32),
+            pltpu.VMEM((2, 1152, W), F32),
+            pltpu.VMEM((2, 8, 3, LAYERS, W), F32),
             pltpu.VMEM((2, 2, 192, W), F32),
             pltpu.VMEM((192, 512), BF16),
             dma((len(args),)),

time: 27.3 us -> 26.1 us (0.956)
  the two profiles are of different devices: /device:TPU:6 before, /device:TPU:1 now
where the time goes in v4:
time: 26.1 us; the launch traced here: 25.8 us
  Pallas kernels  25 us (96%)
  local copies, waits for them, and re-layouts  0.8 us (3%)
    pallas_call x1, Pallas kernels, slot(): pl.pallas_call(functools.partial(slot_kernel, cells), out_shape=pltpu.VME...  25 us
    unnamed x1, local copies, waits for them, and re-layouts  0.8 us

profile of v4, /device:TPU:1, one launch (start us, length us, event | category | flops | bytes accessed | tf_op | source)
XLA Modules:
  0.0 25.8 jit_solution(17240400085455741958)
XLA Ops:
  0.0 25.0 %slot.1 = f32[1024,128]{1,0:T(8,128)S(1)} custom-call(f32[8,2,16,256]{3,2,1,0:T(8,128)} %bitcast.12, bf16[32,2,3072]{2,1,0:T(2,128)(2,1)} %bitcast.11, s32[1,256]{1,0:T(1,128)} %lay_any.1, s32[16,256]{1,0:T(8,128)} %bitcast.13, f32[1,128]{1,0:T(1,128)} %power_any.1, s32[6,32]{1,0:T(8,128)} %bitcast.14, f32[6,32]{1,0:T(8,128)} %bitcast.15, ...), custom_call_target="tpu_custom_call" | custom-call | tf_op jit(solution)/shard_map/slot/pallas_call | solution.py:562
  25.0 0.8 %copy.12 = f32[1,8,2,2,4096]{4,3,2,1,0:T(2,128)} copy(f32[1,8,2,2,4096]{4,3,2,1,0:T(2,128)S(1)} %bitcast.10) | data formatting | bytes 1048576

commit v5 on v4

--- a/solution.py
+++ b/solution.py
@@ -386,16 +386,21 @@
         ecol[2, j] = ecol[0, j] + ecol[1, j]
         scol[2, j] = scol[0, j] + scol[1, j]
 
-    def product(ref):
-        sums = [[jnp.zeros((LAYERS, W), F32) for j in range(4)] for c in range(3)]
-        for k in range(LAYERS):
-            for c in range(3):
+    def products(refs):
+        sums = [[[jnp.zeros((LAYERS, W), F32) for j in range(4)] for c in range(3)] for _ in refs]
+        for c in range(3):
+            for k in range(LAYERS):
                 left = ea[c, k]
-                for j in range(4):
-                    sums[c][j] = sums[c][j] + left * ref[c, j, k : k + 1, :]
-        real = [sums[0][j] - sums[1][j] for j in range(4)]
-        imag = [sums[2][j] - (sums[0][j] + sums[1][j]) for j in range(4)]
-        return real, imag
+                for ref, held in zip(refs, sums):
+                    for j in range(4):
+                        held[c][j] = held[c][j] + left * ref[c, j, k : k + 1, :]
+        return [
+            (
+                [held[0][j] - held[1][j] for j in range(4)],
+                [held[2][j] - (held[0][j] + held[1][j]) for j in range(4)],
+            )
+            for held in sums
+        ]
 
     def put_square(square):
         for c in range(2):
@@ -403,17 +408,17 @@
                 ecol[c, j] = square[c][j]
         for j in range(4):
             ecol[2, j] = square[0][j] + square[1][j]
-        for c in range(3):
-            for j in range(4):
-                full = spread4(ecol[c, j])
-                for g in range(4):
-                    ea[c, 4 * j + g] = full[g]
-
-    put_square(product(ecol))
+        for j in range(4):
+            real, imag = spread4(square[0][j]), spread4(square[1][j])
+            for g in range(4):
+                ea[0, 4 * j + g] = real[g]
+                ea[1, 4 * j + g] = imag[g]
+                ea[2, 4 * j + g] = real[g] + imag[g]
+
+    put_square(products([ecol])[0])
 
     def level(i, _):
-        more = product(scol)
-        square = product(ecol)
+        more, square = products([scol, ecol])
         for j in range(4):
             for c in range(2):
                 scol[c, j] = scol[c, j] + more[c][j]
@@ -422,30 +427,31 @@
         return _
 
     lax.fori_loop(1, 5, level, 0)
-    more = product(scol)
+    (more,) = products([scol])
     for j in range(4):
         last = [(scol[c, j] + more[c][j]) * inv_trace for c in range(2)]
-        for c, part in enumerate(last + [last[0] + last[1]]):
-            full = spread4(part)
-            for g in range(4):
-                ea[c, 4 * j + g] = full[g]
+        real, imag = spread4(last[0]), spread4(last[1])
+        for g in range(4):
+            ea[0, 4 * j + g] = real[g]
+            ea[1, 4 * j + g] = imag[g]
+            ea[2, 4 * j + g] = real[g] + imag[g]
 
     def apply_step(z, energy):
-        sums = [[jnp.zeros((LAYERS, W), F32) for c in range(3)] for ah in range(2)]
-        for m in range(LAYERS):
-            for c in range(3):
+        sums = [[jnp.zeros((LAYERS, W), F32) for c in range(3)] for a in range(4)]
+        for c in range(3):
+            for m in range(LAYERS):
                 right = ea[c, m]
-                for ah in range(2):
-                    sums[ah][c] = sums[ah][c] + hb[2 * z + ah, c, m : m + 1, :] * right
-        for ah in range(2):
-            vr = sums[ah][0] - sums[ah][1]
-            vi = (sums[ah][0] + sums[ah][1]) - sums[ah][2]
-            vs[2 * z + ah, 0] = vr
-            vs[2 * z + ah, 1] = vi
+                for a in range(4):
+                    sums[a][c] = sums[a][c] + hb[4 * z + a, c, m : m + 1, :] * right
+        for a in range(4):
+            vr = sums[a][0] - sums[a][1]
+            vi = (sums[a][0] + sums[a][1]) - sums[a][2]
+            vs[4 * z + a, 0] = vr
+            vs[4 * z + a, 1] = vi
             energy = energy + (vr * vr + vi * vi)
         return energy
 
-    energy = total4(lax.fori_loop(0, LANES, apply_step, jnp.zeros((LAYERS, W), F32)))
+    energy = total4(lax.fori_loop(0, LANES // 2, apply_step, jnp.zeros((LAYERS, W), F32)))
     scale = own_amp / jnp.sqrt(energy + NORM_EPS)
 
     def round_block(z, target):
@@ -513,7 +519,7 @@
     fetches[7].wait()
     fetches[8].wait()
 
-    def section(nt, _):
+    def section(nt):
         result = jnp.dot(lhs[...], dft[nt], preferred_element_type=F32)
         for s in range(SYMS):
             part = [[None, None] for _ in range(4)]
@@ -532,9 +538,13 @@
             for n2 in range(4):
                 for c in range(2):
                     out[pl.ds(c * 64 + (n2 * 8 + nt) * 2 + s, 8, stride=128), :] = outs[n2][c]
+
+    def sections(i, _):
+        for step in range(4):
+            section(4 * i + step)
         return _
 
-    lax.fori_loop(0, 8, section, 0)
+    lax.fori_loop(0, 2, sections, 0)
 
 
 def ofdm_tables():

time: 26.1 us -> 24.9 us (0.954)
  Pallas kernels: 25 us -> 23.8 us
    pallas_call x1, Pallas kernels: 25 us -> 23.8 us  [slot(): pl.pallas_call(functools.partial(slot_kernel, cells), out_shape=pltpu.VME...]
where the time goes in v5:
time: 24.9 us; the launch traced here: 24.6 us
  Pallas kernels  23.8 us (96%)
  local copies, waits for them, and re-layouts  0.8 us (3%)
    pallas_call x1, Pallas kernels, slot(): pl.pallas_call(functools.partial(slot_kernel, cells), out_shape=pltpu.VME...  23.8 us
    unnamed x1, local copies, waits for them, and re-layouts  0.8 us

profile of v5, /device:TPU:1, one launch (start us, length us, event | category | flops | bytes accessed | tf_op | source)
XLA Modules:
  0.0 24.6 jit_solution(8553661004652582918)
XLA Ops:
  0.0 23.8 %slot.1 = f32[1024,128]{1,0:T(8,128)S(1)} custom-call(f32[8,2,16,256]{3,2,1,0:T(8,128)} %bitcast.12, bf16[32,2,3072]{2,1,0:T(2,128)(2,1)} %bitcast.11, s32[1,256]{1,0:T(1,128)} %lay_any.1, s32[16,256]{1,0:T(8,128)} %bitcast.13, f32[1,128]{1,0:T(1,128)} %power_any.1, s32[6,32]{1,0:T(8,128)} %bitcast.14, f32[6,32]{1,0:T(8,128)} %bitcast.15, ...), custom_call_target="tpu_custom_call" | custom-call | tf_op jit(solution)/shard_map/slot/pallas_call | solution.py:572
  23.8 0.8 %copy.12 = f32[1,8,2,2,4096]{4,3,2,1,0:T(2,128)} copy(f32[1,8,2,2,4096]{4,3,2,1,0:T(2,128)S(1)} %bitcast.10) | data formatting | bytes 1048576

commit v6 on v5

--- a/solution.py
+++ b/solution.py
@@ -165,10 +165,11 @@
 def slot_kernel(
     cells, ch_any, sym_any, lay_any, uid_any, power_any, neigh_any, coup_any, dft_any, twist_any, out,
     ch, sym, lay, uid, power, neigh, coup, dft, twist,
-    sb, rb, hb, amp, lay_all, wsf, wrf, tx_own, tx_all, sig_all, sig_in, ea, ecol, scol, vs, wsb, w_out,
+    sb, rb, hb, amp, lay_all, wsf, wrf, tx_own, tx_all, sig_all, sig_in, eas, ecol, scol, vs, wsb, w_out,
     symf, tmp, sy, wn, gf, lhs,
     ins, hs, hr, ts, tr, ss, sr, ws, wr, ready,
 ):
+    ea, eb = eas.at[0], eas.at[1]
     fetches = [
         pltpu.make_async_copy(source, held, ins.at[i])
         for i, (source, held) in enumerate((
@@ -386,11 +387,11 @@
         ecol[2, j] = ecol[0, j] + ecol[1, j]
         scol[2, j] = scol[0, j] + scol[1, j]
 
-    def products(refs):
+    def products(refs, held_in):
         sums = [[[jnp.zeros((LAYERS, W), F32) for j in range(4)] for c in range(3)] for _ in refs]
         for c in range(3):
             for k in range(LAYERS):
-                left = ea[c, k]
+                left = held_in[c, k]
                 for ref, held in zip(refs, sums):
                     for j in range(4):
                         held[c][j] = held[c][j] + left * ref[c, j, k : k + 1, :]
@@ -402,7 +403,7 @@
             for held in sums
         ]
 
-    def put_square(square):
+    def put_square(square, to):
         for c in range(2):
             for j in range(4):
                 ecol[c, j] = square[c][j]
@@ -411,23 +412,24 @@
         for j in range(4):
             real, imag = spread4(square[0][j]), spread4(square[1][j])
             for g in range(4):
-                ea[0, 4 * j + g] = real[g]
-                ea[1, 4 * j + g] = imag[g]
-                ea[2, 4 * j + g] = real[g] + imag[g]
-
-    put_square(products([ecol])[0])
+                to[0, 4 * j + g] = real[g]
+                to[1, 4 * j + g] = imag[g]
+                to[2, 4 * j + g] = real[g] + imag[g]
+
+    put_square(products([ecol], ea)[0], eb)
 
     def level(i, _):
-        more, square = products([scol, ecol])
-        for j in range(4):
-            for c in range(2):
-                scol[c, j] = scol[c, j] + more[c][j]
-            scol[2, j] = scol[0, j] + scol[1, j]
-        put_square(square)
+        for held_in, to in ((eb, ea), (ea, eb)):
+            put_square(products([ecol], held_in)[0], to)
+            (more,) = products([scol], held_in)
+            for j in range(4):
+                for c in range(2):
+                    scol[c, j] = scol[c, j] + more[c][j]
+                scol[2, j] = scol[0, j] + scol[1, j]
         return _
 
-    lax.fori_loop(1, 5, level, 0)
-    (more,) = products([scol])
+    lax.fori_loop(0, 2, level, 0)
+    (more,) = products([scol], eb)
     for j in range(4):
         last = [(scol[c, j] + more[c][j]) * inv_trace for c in range(2)]
         real, imag = spread4(last[0]), spread4(last[1])
@@ -586,7 +588,7 @@
             pltpu.VMEM((cells, 2, W), F32),
             pltpu.VMEM((LANES, 1, W), F32),
             pltpu.VMEM((1, W), F32),
-            pltpu.VMEM((3, LAYERS, LAYERS, W), F32),
+            pltpu.VMEM((2, 3, LAYERS, LAYERS, W), F32),
             pltpu.VMEM((3, 4, LAYERS, W), F32),
             pltpu.VMEM((3, 4, LAYERS, W), F32),
             pltpu.VMEM(block, F32),

time: 24.9 us -> 24.7 us (level)
  no operation moved by 1% of the time
where the time goes in v6:
time: 24.7 us; the launch traced here: 24.4 us
  Pallas kernels  23.6 us (96%)
  local copies, waits for them, and re-layouts  0.8 us (3%)
    pallas_call x1, Pallas kernels, slot(): pl.pallas_call(functools.partial(slot_kernel, cells), out_shape=pltpu.VME...  23.6 us
    unnamed x1, local copies, waits for them, and re-layouts  0.8 us

profile of v6, /device:TPU:1, one launch (start us, length us, event | category | flops | bytes accessed | tf_op | source)
XLA Modules:
  0.0 24.4 jit_solution(707763792230318856)
XLA Ops:
  0.0 23.6 %slot.1 = f32[1024,128]{1,0:T(8,128)S(1)} custom-call(f32[8,2,16,256]{3,2,1,0:T(8,128)} %bitcast.12, bf16[32,2,3072]{2,1,0:T(2,128)(2,1)} %bitcast.11, s32[1,256]{1,0:T(1,128)} %lay_any.1, s32[16,256]{1,0:T(8,128)} %bitcast.13, f32[1,128]{1,0:T(1,128)} %power_any.1, s32[6,32]{1,0:T(8,128)} %bitcast.14, f32[6,32]{1,0:T(8,128)} %bitcast.15, ...), custom_call_target="tpu_custom_call" | custom-call | tf_op jit(solution)/shard_map/slot/pallas_call | solution.py:574
  23.6 0.8 %copy.12 = f32[1,8,2,2,4096]{4,3,2,1,0:T(2,128)} copy(f32[1,8,2,2,4096]{4,3,2,1,0:T(2,128)S(1)} %bitcast.10) | data formatting | bytes 1048576
